TPU v7x, 32 devices: a whole 2x2x4 slice. The times are simulated.
32 devices in a mesh: seq: 8 (over z, y), head: 4 (over x, core).
Axes of the slice: x: 2, y: 2, z: 4, core: 2. Of those that a mesh axis runs over, the one named last changes fastest.
Arguments:
- tokens: bfloat16 [2048, 1024], P('seq'), may hold values from -6 to 6
- w_qkv: bfloat16 [1024, 3, 1024], P('seq', None, 'head'), may hold values from -0.1875 to 0.1875
- w_out: bfloat16 [1024, 1024], P('head', 'seq'), may hold values from -1 to 1
- ln1_gain: bfloat16 [1024], P('seq'), may hold values from 0.5 to 1.5
- ln1_bias: bfloat16 [1024], P('seq'), may hold values from -1.796875 to 1.796875
- ln2_gain: bfloat16 [1024], P('seq'), may hold values from 0.5 to 1.5
- ln2_bias: bfloat16 [1024], P('seq'), may hold values from -1.796875 to 1.796875
- w_up: bfloat16 [1024, 4096], P('seq', 'head'), may hold values from -0.1875 to 0.1875
- up_bias: bfloat16 [4096], P('head'), may hold values from -1.796875 to 1.796875
- w_down: bfloat16 [4096, 1024], P('head', 'seq'), may hold values from -0.09375 to 0.09375
- down_bias: bfloat16 [1024], P('seq'), may hold values from -1.796875 to 1.796875
- seq_units: int32 [4], replicated, may hold values from 1 to 4, 8 in all
- seq_pad: int32 [4], replicated, may hold values from 0 to 127
- rand_picks: int32 [32, 16, 3], P('seq', 'head'), may hold values from 0 to 65535
- cotangent: bfloat16 [2048, 1024], P('seq'), may hold values from -6 to 6
Outputs:
- output: bfloat16 [2048, 1024], P('seq')
- x_grad: float32 [2048, 1024], P('seq')
- w_qkv_grad: float32 [1024, 3, 1024], P('seq', None, 'head')
- w_out_grad: float32 [1024, 1024], P('head', 'seq')
- ln1_gain_grad: float32 [1024], P('seq')
- ln1_bias_grad: float32 [1024], P('seq')
- ln2_gain_grad: float32 [1024], P('seq')
- ln2_bias_grad: float32 [1024], P('seq')
- w_up_grad: float32 [1024, 4096], P('seq', 'head')
- up_bias_grad: float32 [4096], P('head')
- w_down_grad: float32 [4096, 1024], P('head', 'seq')
- down_bias_grad: float32 [1024], P('seq')
Inputs may be any that keep to these rules, and one draw needn't show every extreme that they name: `seq_units`: each sequence covers whole units; the values add up to the number of units in the stream, and some sequence covers 4 units.
All inputs are finite; a program needn't handle non-finite values.
Results may differ from a plain program's by a relative error of at most 0.012.
Values may be sent and summed in bfloat16 or wider, within the bound.
A program may use at most 128 MiB of HBM per device.

v0:
```python
import jax
import jax.numpy as jnp
from jax import lax
from jax.sharding import PartitionSpec as P

HEAD_DIM = 64
BLK = 64
SPAN = 4
BLK_DEV = 4
EPSILON = 1e-05
NEGATIVE = -1e30
F32 = jnp.float32
BF16 = jnp.bfloat16


def shifted(value, axis, steps):
    count = lax.axis_size(axis)
    first, last = (max(0, -steps), min(count, count - steps))
    return lax.ppermute(value, axis, [(i, i + steps) for i in range(first, last)])


def norm_parts(features):
    average = jnp.mean(features, axis=-1, keepdims=True)
    centred = features - average
    spread = jnp.mean(centred * centred, axis=-1, keepdims=True)
    inverse = lax.rsqrt(spread + EPSILON)
    return (centred * inverse, inverse)


def norm_backward(xhat, inverse, scaled):
    first = jnp.mean(scaled, axis=-1, keepdims=True)
    second = jnp.mean(scaled * xhat, axis=-1, keepdims=True)
    return inverse * (scaled - first - xhat * second)


def dot(a, b, dims):
    return lax.dot_general(a, b, (dims, ((), ())), preferred_element_type=F32)


def sequence_place(seq_units, seq_pad):
    device = lax.axis_index("seq")
    start, leader, span, pad = (0, 0, 0, 0)
    for k in range(seq_units.shape[0]):
        units = seq_units[k]
        inside = (device >= start) & (device < start + units)
        leader = jnp.where(inside, start, leader)
        span = jnp.where(inside, units, span)
        pad = jnp.where(inside, seq_pad[k], pad)
        start = start + units
    return (device - leader, span, pad)


def key_counts(position, span, picks):
    blocks = lax.broadcasted_iota(jnp.int32, (1, 1, SPAN * BLK_DEV), 2)
    query = position * BLK_DEV + lax.broadcasted_iota(jnp.int32, (BLK_DEV, 1, 1), 0)
    total = span * BLK_DEV
    count = jnp.zeros((BLK_DEV, picks.shape[1], SPAN * BLK_DEV), F32)
    for wanted in (query - 1, query, query + 1, 0, total - 1):
        count = count + (blocks == wanted).astype(F32)
    chosen = picks % total
    for r in range(picks.shape[2]):
        count = count + (blocks == chosen[:, :, r : r + 1]).astype(F32)
    return jnp.where((query == 0) | (query == total - 1), 1.0, count)


def local_general(
    tokens,
    w_qkv,
    w_out,
    ln1_gain,
    ln1_bias,
    ln2_gain,
    ln2_bias,
    w_up,
    up_bias,
    w_down,
    down_bias,
    seq_units,
    seq_pad,
    rand_picks,
    cotangent,
):
    tok, width = tokens.shape
    heads = w_qkv.shape[2] // HEAD_DIM
    rows = lambda v: lax.all_gather(v, "seq", axis=0, tiled=True)
    cols = lambda v: lax.all_gather(v, "seq", axis=1, tiled=True)
    vectors = jnp.stack([ln1_gain, ln1_bias, ln2_gain, ln2_bias, down_bias], axis=0)
    gain_one, shift_one, gain_two, shift_two, down_shift = [
        v[None].astype(F32) for v in cols(vectors)
    ]
    qkv = rows(w_qkv)
    out_w, up_w, down_w = (cols(w_out), rows(w_up), cols(w_down))
    position, span, pad = sequence_place(seq_units, seq_pad)
    root = SPAN - 1 - position
    inputs = tokens.astype(F32)
    xhat_one, inv_one = norm_parts(inputs)
    normed = (xhat_one * gain_one + shift_one).astype(BF16)
    triple = jnp.einsum("td,dcf->tcf", normed, qkv, preferred_element_type=F32).astype(BF16)
    own = jnp.stack([triple[:, 1], triple[:, 2]], axis=0)
    pieces = [own if o == 0 else shifted(own, "seq", -o) for o in range(1 - SPAN, SPAN)]
    nearby = jnp.stack(pieces, axis=0)
    window = lax.dynamic_slice_in_dim(nearby, root, SPAN, 0)
    split = lambda v: v.reshape(v.shape[0], heads, HEAD_DIM)
    keys = split(window[:, 0].reshape(SPAN * tok, -1))
    values = split(window[:, 1].reshape(SPAN * tok, -1))
    queries = split(triple[:, 0])
    scaling = HEAD_DIM ** (-0.5)
    live = jnp.arange(SPAN * tok, dtype=jnp.int32) < span * tok - pad
    count = jnp.repeat(key_counts(position, span, rand_picks), BLK, axis=2)
    count = jnp.where(live[None, None], count, 0.0)
    count = jnp.transpose(jnp.repeat(count, BLK, axis=0), (1, 0, 2))
    logits = jnp.einsum("qhd,khd->hqk", queries, keys, preferred_element_type=F32) * scaling
    logits = jnp.where(count > 0, logits, NEGATIVE)
    grown = jnp.exp(logits - jnp.max(logits, axis=-1, keepdims=True)) * count
    chances = grown / jnp.sum(grown, axis=-1, keepdims=True)
    chances_low = chances.astype(BF16)
    attended = jnp.einsum("hqk,khd->qhd", chances_low, values, preferred_element_type=F32)
    attended = attended.astype(BF16).reshape(tok, heads * HEAD_DIM)
    middle = inputs + lax.psum(dot(attended, out_w, ((1,), (0,))), "head")
    xhat_two, inv_two = norm_parts(middle)
    normed_two = (xhat_two * gain_two + shift_two).astype(BF16)
    pre_act = dot(normed_two, up_w, ((1,), (0,))) + up_bias.astype(F32)[None]
    hidden, pull = jax.vjp(lambda v: jax.nn.gelu(v, approximate=True), pre_act)
    hidden = hidden.astype(BF16)
    ffn = lax.psum(dot(hidden, down_w, ((1,), (0,))).astype(BF16), "head").astype(F32)
    output = (middle + ffn + down_shift).astype(BF16)
    grad_out = cotangent.astype(F32)
    grad_w_down = dot(hidden, cotangent, ((0,), (0,)))
    grad_pre = pull(dot(cotangent, down_w, ((1,), (1,))))[0].astype(BF16)
    grad_w_up = dot(normed_two, grad_pre, ((0,), (0,)))
    grad_up_bias = lax.psum(jnp.sum(grad_pre.astype(F32), axis=0), "seq")
    grad_two = lax.psum(dot(grad_pre, up_w, ((1,), (1,))), "head")
    grad_middle = grad_out + norm_backward(xhat_two, inv_two, grad_two * gain_two)
    grad_branch = grad_middle.astype(BF16)
    grad_w_out = dot(attended, grad_branch, ((0,), (0,)))
    grad_att = split(dot(grad_branch, out_w, ((1,), (1,))).astype(BF16))
    grad_prob = jnp.einsum("qhd,khd->hqk", grad_att, values, preferred_element_type=F32)
    inner = jnp.sum(chances * grad_prob, axis=-1, keepdims=True)
    grad_logit = (chances * (grad_prob - inner)).astype(BF16)
    dq = scaling * jnp.einsum("hqk,khd->qhd", grad_logit, keys, preferred_element_type=F32)
    dk = scaling * jnp.einsum("hqk,qhd->khd", grad_logit, queries, preferred_element_type=F32)
    dv = jnp.einsum("hqk,qhd->khd", chances_low, grad_att, preferred_element_type=F32)
    part = jnp.stack([dk.reshape(SPAN, tok, -1), dv.reshape(SPAN, tok, -1)], axis=1)
    near = jnp.zeros((2 * SPAN - 1,) + part.shape[1:], F32)
    near = lax.dynamic_update_slice_in_dim(near, part, root, 0)
    owned = near[SPAN - 1]
    for offset in range(1 - SPAN, SPAN):
        if offset:
            owned = owned + shifted(near[offset + SPAN - 1], "seq", offset)
    owned = owned.astype(BF16)
    grad_triple = jnp.stack([dq.reshape(tok, -1).astype(BF16), owned[0], owned[1]], axis=1)
    grad_w_qkv = jnp.einsum("td,tcf->dcf", normed, grad_triple, preferred_element_type=F32)
    grad_one = lax.psum(
        jnp.einsum("tcf,dcf->td", grad_triple, qkv, preferred_element_type=F32), "head"
    )
    x_grad = grad_middle + norm_backward(xhat_one, inv_one, grad_one * gain_one)
    sums = jnp.stack(
        [
            jnp.sum(grad_one * xhat_one, axis=0),
            jnp.sum(grad_one, axis=0),
            jnp.sum(grad_two * xhat_two, axis=0),
            jnp.sum(grad_two, axis=0),
            jnp.sum(grad_out, axis=0),
        ],
        axis=0,
    )
    scatter = lambda v, d: lax.psum_scatter(v, "seq", scatter_dimension=d, tiled=True)
    sums = scatter(sums, 1)
    return (
        output,
        x_grad,
        scatter(grad_w_qkv, 0),
        scatter(grad_w_out, 1),
        sums[0],
        sums[1],
        sums[2],
        sums[3],
        scatter(grad_w_up, 0),
        grad_up_bias,
        scatter(grad_w_down, 1),
        sums[4],
    )


IN_SPECS = (
    P("seq", None),
    P("seq", None, "head"),
    P("head", "seq"),
    P("seq"),
    P("seq"),
    P("seq"),
    P("seq"),
    P("seq", "head"),
    P("head"),
    P("head", "seq"),
    P("seq"),
    P(),
    P(),
    P("seq", "head", None),
    P("seq", None),
)
OUT_SPECS = (
    P("seq", None),
    P("seq", None),
    P("seq", None, "head"),
    P("head", "seq"),
    P("seq"),
    P("seq"),
    P("seq"),
    P("seq"),
    P("seq", "head"),
    P("head"),
    P("head", "seq"),
    P("seq"),
)


def solution(mesh):
    return jax.shard_map(
        local_general, mesh=mesh, in_specs=IN_SPECS, out_specs=OUT_SPECS, check_vma=False
    )
```

profile of v0, /device:TPU:0, one launch (start us, length us, event | category | flops | bytes accessed | tf_op | source)
XLA Modules:
  0.0 851.5 jit_solution(9352380124314227854)
XLA Ops:
  23.5 27.9 %all_gather.15 = bf16[5,1024]{1,0:T(8,128)(2,1)S(1)} all-gather(bf16[5,128]{1,0:T(8,128)(2,1)S(1)} %stack.75), channel_id=1, replica_groups=mesh['seq'=8,'head'=4] {'seq'}, dimensions={1}, use_global_device_ids=true | all-gather | bytes 11520 | tf_op jit(solution)/shard_map/all_gather | solution.py:86
  54.2 27.8 %all_gather.17 = bf16[256,1024]{1,0:T(8,128)(2,1)S(1)} all-gather(bf16[256,128]{1,0:T(8,128)(2,1)} %param.17), channel_id=1, replica_groups=mesh['seq'=8,'head'=4] {'seq'}, dimensions={1}, use_global_device_ids=true | all-gather | bytes 589824 | tf_op jit(solution)/shard_map/all_gather | solution.py:86
  86.1 5.1 collective-permute-start.1
  96.8 4.2 collective-permute-done.3
  101.0 6.9 collective-permute-done.4
  109.7 2.9 fusion.49
  113.3 3.2 convolution_convert_fusion.3
  119.3 38.9 %all-reduce.5.cloned.1.call-done = f32[256,1024]{1,0:T(8,128)} async-done(((f32[256,1024]{1,0:T(8,128)}), f32[256,1024]{1,0:T(8,128)}) %all-reduce.5.cloned.1.call-update) | async-done | bytes 1048592 | tf_op jit(solution)/shard_map/psum | solution.py:119
  159.9 52.1 %all-gather.8.cloned.1.call-done = bf16[1024,1024]{1,0:T(8,128)(2,1)} async-done(((bf16[1024,128]{1,0:T(8,128)(2,1)}), bf16[1024,1024]{1,0:T(8,128)(2,1)}) %all-gather.8.cloned.1.call-update) | async-done | bytes 2097168 | tf_op jit(solution)/shard_map/all_gather | solution.py:86
  211.9 3.3 fusion.51
  215.2 46.4 %all-gather.6.cloned.1.call-done = bf16[1024,1024]{1,0:T(8,128)(2,1)} async-done(((bf16[128,1024]{1,0:T(8,128)(2,1)}), bf16[1024,1024]{1,0:T(8,128)(2,1)}) %all-gather.6.cloned.1.call-update) | async-done | bytes 2097168 | tf_op jit(solution)/shard_map/all_gather | solution.py:85
  261.6 3.5 convert_reduce_fusion.2
  267.8 3.2 convolution_convert_fusion
  271.2 31.2 %all-reduce.9.cloned.1.call-done = f32[256,1024]{1,0:T(8,128)} async-done(((f32[256,1024]{1,0:T(8,128)}), f32[256,1024]{1,0:T(8,128)}) %all-reduce.9.cloned.1.call-update) | async-done | bytes 1048592 | tf_op jit(solution)/shard_map/psum | solution.py:132
  304.2 34.6 %all-reduce.7.cloned.1.call-done = bf16[256,1024]{1,0:T(8,128)(2,1)} async-done(((bf16[256,1024]{1,0:T(8,128)(2,1)}), bf16[256,1024]{1,0:T(8,128)(2,1)}) %all-reduce.7.cloned.1.call-update) | async-done | bytes 524304 | tf_op jit(solution)/shard_map/psum | solution.py:125
  338.8 2.9 convert_add_fusion.1
  363.6 4.2 collective-permute-start.10
  367.8 4.3 collective-permute-start.11
  375.9 3.4 collective-permute-done.10
  379.3 4.2 collective-permute-start.9
  384.4 11.5 %collective-permute-done.11 = f32[2,256,256]{2,1,0:T(8,128)} collective-permute-done((f32[2,256,256]{2,1,0:T(8,128)}, f32[2,256,256]{2,1,0:T(8,128)}, u32[]{:S(2)}, u32[]{:S(2)}) %collective-permute-start.11) | collective-permute-done | bytes 524320 | tf_op jit(solution)/shard_map/ppermute | solution.py:19
  395.9 5.4 collective-permute-done.7
  401.3 10.7 %collective-permute-done.9 = f32[2,256,256]{2,1,0:T(8,128)} collective-permute-done((f32[2,256,256]{2,1,0:T(8,128)}, f32[2,256,256]{2,1,0:T(8,128)}, u32[]{:S(2)}, u32[]{:S(2)}) %collective-permute-start.9) | collective-permute-done | bytes 524320 | tf_op jit(solution)/shard_map/ppermute | solution.py:19
  415.9 41.7 %all-reduce.11.cloned.1.call-done = f32[256,1024]{1,0:T(8,128)} async-done(((f32[256,1024]{1,0:T(8,128)}), f32[256,1024]{1,0:T(8,128)}) %all-reduce.11.cloned.1.call-update) | async-done | bytes 1048592 | tf_op jit(solution)/shard_map/psum | solution.py:153
  465.0 2.8 fusion.43
  469.2 2.9 fusion.42
  472.1 22.1 %psum.39 = f32[1024]{0:T(1024)} all-reduce(f32[1024]{0:T(1024)S(1)} %get-tuple-element.20), channel_id=1, replica_groups=mesh['seq'=8,'head'=4] {'seq'}, use_global_device_ids=true, to_apply=%region_25.26 | all-reduce | flops 1024 | bytes 8192 | tf_op jit(solution)/shard_map/psum | solution.py:131
  495.5 19.4 %reduce-scatter.10.cloned.1.call-done = f32[5,128]{1,0:T(8,128)} async-done(((f32[5,1024]{1,0:T(8,128)}), f32[5,128]{1,0:T(8,128)}) %reduce-scatter.10.cloned.1.call-update) | async-done | bytes 2576 | tf_op jit(solution)/shard_map/reduce_scatter | solution.py:167
  516.3 65.9 %reduce-scatter.8.cloned.1.call-done = f32[256,128]{1,0:T(8,128)} async-done(((f32[256,1024]{1,0:T(8,128)}), f32[256,128]{1,0:T(8,128)}) %reduce-scatter.8.cloned.1.call-update) | async-done | bytes 131088 | tf_op jit(solution)/shard_map/reduce_scatter | solution.py:167
  582.2 78.2 %reduce-scatter.6.cloned.1.call-done = f32[128,3,256]{2,0,1:T(8,128)} async-done(((f32[1024,3,256]{2,0,1:T(8,128)}), f32[128,3,256]{2,0,1:T(8,128)}) %reduce-scatter.6.cloned.1.call-update) | async-done | bytes 393232 | tf_op jit(solution)/shard_map/reduce_scatter | solution.py:167
  660.4 91.4 %reduce-scatter.12.cloned.1.call-done = f32[128,1024]{1,0:T(8,128)} async-done(((f32[1024,1024]{1,0:T(8,128)}), f32[128,1024]{1,0:T(8,128)}) %reduce-scatter.12.cloned.1.call-update) | async-done | bytes 524304 | tf_op jit(solution)/shard_map/reduce_scatter | solution.py:167
  751.8 92.8 %reduce-scatter.14.cloned.1.call-done = f32[1024,128]{1,0:T(8,128)} async-done(((f32[1024,1024]{1,0:T(8,128)}), f32[1024,128]{1,0:T(8,128)}) %reduce-scatter.14.cloned.1.call-update) | async-done | bytes 524304 | tf_op jit(solution)/shard_map/reduce_scatter | solution.py:167
  (156 shorter events, 71.9 us)
Async XLA Ops:
  7.2 74.8 %copy-start = (bf16[256,1024]{1,0:T(8,128)(2,1)S(1)}, bf16[256,1024]{1,0:T(8,128)(2,1)}, u32[]{:S(2)}) copy-start(bf16[256,1024]{1,0:T(8,128)(2,1)} %param.15) | copy-start | bytes 1572868
  7.2 74.8 %all-gather.4.cloned.1.call-start = ((), (), s32[]{:S(2)}) async-start(), calls=%async_computation.5 | async-start | bytes 1769472 | tf_op jit(solution)/shard_map/all_gather | solution.py:85
  9.0 149.2 %all-reduce.5.cloned.1.call-start = ((), (), s32[]{:S(2)}) async-start(), calls=%async_computation.6 | async-start | bytes 2097152 | tf_op jit(solution)/shard_map/psum | solution.py:119
  84.2 11.1 %collective-permute-start = (bf16[2,256,256]{1,2,0:T(8,128)(2,1)S(1)}, bf16[2,256,256]{1,2,0:T(8,128)(2,1)S(1)}, u32[]{:S(2)}, u32[]{:S(2)}) collective-permute-start(bf16[2,256,256]{1,2,0:T(8,128)(2,1)S(1)} %pad_maximum_fusion.1), channel_id=1, source_target_pairs={{0,12},{4,16},{8,20},{12,24},{16,28},{1,13},{5,17},{9,21},{13,25},... | collective-permute-start | bytes 786440 | tf_op jit(solution)/shard_map/ppermute | solution.py:19
  86.1 10.6 %collective-permute-start.1 = (bf16[2,256,256]{1,2,0:T(8,128)(2,1)S(1)}, bf16[2,256,256]{1,2,0:T(8,128)(2,1)S(1)}, u32[]{:S(2)}, u32[]{:S(2)}) collective-permute-start(bf16[2,256,256]{1,2,0:T(8,128)(2,1)S(1)} %pad_maximum_fusion.1), channel_id=1, source_target_pairs={{0,8},{4,12},{8,16},{12,20},{16,24},{20,28},{1,9},{5,13},{9,17},{1... | collective-permute-start | bytes 786440 | tf_op jit(solution)/shard_map/ppermute | solution.py:19
  91.3 5.4 collective-permute-start.2
  92.7 8.3 collective-permute-start.3
  94.0 13.9 %collective-permute-start.4 = (bf16[2,256,256]{1,2,0:T(8,128)(2,1)S(1)}, bf16[2,256,256]{1,2,0:T(8,128)(2,1)S(1)}, u32[]{:S(2)}, u32[]{:S(2)}) collective-permute-start(bf16[2,256,256]{1,2,0:T(8,128)(2,1)S(1)} %pad_maximum_fusion.1), channel_id=1, source_target_pairs={{8,0},{12,4},{16,8},{20,12},{24,16},{28,20},{9,1},{13,5},{17,9},{2... | collective-permute-start | bytes 786440 | tf_op jit(solution)/shard_map/ppermute | solution.py:19
  95.3 12.6 %collective-permute-start.5 = (bf16[2,256,256]{1,2,0:T(8,128)(2,1)S(1)}, bf16[2,256,256]{1,2,0:T(8,128)(2,1)S(1)}, u32[]{:S(2)}, u32[]{:S(2)}) collective-permute-start(bf16[2,256,256]{1,2,0:T(8,128)(2,1)S(1)} %pad_maximum_fusion.1), channel_id=1, source_target_pairs={{12,0},{16,4},{20,8},{24,12},{28,16},{13,1},{17,5},{21,9},{25,13},... | collective-permute-start | bytes 786440 | tf_op jit(solution)/shard_map/ppermute | solution.py:19
  117.9 94.0 %copy-start.7 = (bf16[256,1024]{1,0:T(8,128)(2,1)S(1)}, bf16[256,1024]{1,0:T(8,128)(2,1)}, u32[]{:S(2)}) copy-start(bf16[256,1024]{1,0:T(8,128)(2,1)} %param.29) | copy-start | bytes 1572868
  117.9 94.0 %all-gather.8.cloned.1.call-start = ((), (), s32[]{:S(2)}) async-start(), calls=%async_computation.8 | async-start | bytes 2359296 | tf_op jit(solution)/shard_map/all_gather | solution.py:86
  118.6 143.0 %all-gather.6.cloned.1.call-start = ((), (), s32[]{:S(2)}) async-start(), calls=%async_computation.7 | async-start | bytes 2359296 | tf_op jit(solution)/shard_map/all_gather | solution.py:85
  119.2 183.2 %all-reduce.9.cloned.1.call-start = ((), (), s32[]{:S(2)}) async-start(), calls=%async_computation.10 | async-start | bytes 2097152 | tf_op jit(solution)/shard_map/psum | solution.py:132
  261.6 4.3 copy-start.12
  267.7 71.1 %all-reduce.7.cloned.1.call-start = ((), (), s32[]{:S(2)}) async-start(), calls=%async_computation.9 | async-start | bytes 1048576 | tf_op jit(solution)/shard_map/psum | solution.py:125
  271.0 186.6 %all-reduce.11.cloned.1.call-start = ((), (), s32[]{:S(2)}) async-start(), calls=%async_computation.11 | async-start | bytes 2097152 | tf_op jit(solution)/shard_map/psum | solution.py:153
  338.8 3.3 copy-start.19
  360.6 22.9 %copy-start.2 = (bf16[4,256,1024]{2,1,0:T(8,128)(2,1)S(1)}, bf16[4,256,1024]{2,1,0:T(8,128)(2,1)}, u32[]{:S(2)}) copy-start(bf16[4,256,1024]{2,1,0:T(8,128)(2,1)} %copy-done.1) | copy-start | bytes 6291460
  360.6 22.9 %copy-start.6 = (bf16[1024,4,64]{0,2,1:T(8,128)(2,1)S(1)}, bf16[1024,4,64]{0,2,1:T(8,128)(2,1)}, u32[]{:S(2)}) copy-start(bf16[1024,4,64]{0,2,1:T(8,128)(2,1)} %copy-done.5) | copy-start | bytes 1572868
  363.6 15.7 %collective-permute-start.10 = (f32[2,256,256]{2,1,0:T(8,128)S(1)}, f32[2,256,256]{2,1,0:T(8,128)}, u32[]{:S(2)}, u32[]{:S(2)}) collective-permute-start(f32[2,256,256]{2,1,0:T(8,128)S(1)} %get-tuple-element.26), channel_id=1, source_target_pairs={{0,8},{4,12},{8,16},{12,20},{16,24},{20,28},{1,9},{5,13},{9,17},{1... | collective-permute-start | bytes 1572872 | tf_op jit(solution)/shard_map/ppermute | solution.py:19
  367.8 28.1 %collective-permute-start.11 = (f32[2,256,256]{2,1,0:T(8,128)}, f32[2,256,256]{2,1,0:T(8,128)}, u32[]{:S(2)}, u32[]{:S(2)}) collective-permute-start(f32[2,256,256]{2,1,0:T(8,128)} %get-tuple-element.25), channel_id=1, source_target_pairs={{0,12},{4,16},{8,20},{12,24},{16,28},{1,13},{5,17},{9,21},{13,25},... | collective-permute-start | bytes 1572872 | tf_op jit(solution)/shard_map/ppermute | solution.py:19
  372.1 23.9 %collective-permute-start.6 = (f32[2,256,256]{2,1,0:T(8,128)}, f32[2,256,256]{2,1,0:T(8,128)}, u32[]{:S(2)}, u32[]{:S(2)}) collective-permute-start(f32[2,256,256]{2,1,0:T(8,128)} %get-tuple-element.24), channel_id=1, source_target_pairs={{12,0},{16,4},{20,8},{24,12},{28,16},{13,1},{17,5},{21,9},{25,13},... | collective-permute-start | bytes 1572872 | tf_op jit(solution)/shard_map/ppermute | solution.py:19
  373.3 28.0 %collective-permute-start.7 = (f32[2,256,256]{2,1,0:T(8,128)}, f32[2,256,256]{2,1,0:T(8,128)}, u32[]{:S(2)}, u32[]{:S(2)}) collective-permute-start(f32[2,256,256]{2,1,0:T(8,128)} %get-tuple-element.29), channel_id=1, source_target_pairs={{8,0},{12,4},{16,8},{20,12},{24,16},{28,20},{9,1},{13,5},{17,9},{2... | collective-permute-start | bytes 1572872 | tf_op jit(solution)/shard_map/ppermute | solution.py:19
  374.6 26.7 %collective-permute-start.8 = (f32[2,256,256]{2,1,0:T(8,128)}, f32[2,256,256]{2,1,0:T(8,128)}, u32[]{:S(2)}, u32[]{:S(2)}) collective-permute-start(f32[2,256,256]{2,1,0:T(8,128)} %get-tuple-element.28), channel_id=1, source_target_pairs={{4,0},{8,4},{12,8},{16,12},{20,16},{24,20},{28,24},{5,1},{9,5},{13... | collective-permute-start | bytes 1572872 | tf_op jit(solution)/shard_map/ppermute | solution.py:19
  379.3 32.7 %collective-permute-start.9 = (f32[2,256,256]{2,1,0:T(8,128)}, f32[2,256,256]{2,1,0:T(8,128)}, u32[]{:S(2)}, u32[]{:S(2)}) collective-permute-start(f32[2,256,256]{2,1,0:T(8,128)} %get-tuple-element.27), channel_id=1, source_target_pairs={{0,4},{4,8},{8,12},{12,16},{16,20},{20,24},{24,28},{1,5},{5,9},{9,... | collective-permute-start | bytes 1572872 | tf_op jit(solution)/shard_map/ppermute | solution.py:19
  384.4 29.9 %copy-start.15 = (bf16[1024,3,256]{0,2,1:T(8,128)(2,1)S(1)}, bf16[1024,3,256]{0,2,1:T(8,128)(2,1)}, u32[]{:S(2)}) copy-start(bf16[1024,3,256]{0,2,1:T(8,128)(2,1)} %all-gather.4.cloned.1.call-done) | copy-start | bytes 4718596
  415.9 99.1 %reduce-scatter.10.cloned.1.call-start = ((), (), s32[]{:S(2)}) async-start(), calls=%async_computation.14 | async-start | bytes 36864 | tf_op jit(solution)/shard_map/reduce_scatter | solution.py:167
  460.0 122.2 %reduce-scatter.8.cloned.1.call-start = ((), (), s32[]{:S(2)}) async-start(), calls=%async_computation.13 | async-start | bytes 1179648 | tf_op jit(solution)/shard_map/reduce_scatter | solution.py:167
  461.4 199.0 %reduce-scatter.6.cloned.1.call-start = ((), (), s32[]{:S(2)}) async-start(), calls=%async_computation.12 | async-start | bytes 3538944 | tf_op jit(solution)/shard_map/reduce_scatter | solution.py:167
  464.0 287.9 %reduce-scatter.12.cloned.1.call-start = ((), (), s32[]{:S(2)}) async-start(), calls=%async_computation.15 | async-start | bytes 4718592 | tf_op jit(solution)/shard_map/reduce_scatter | solution.py:167
  467.8 376.8 %reduce-scatter.14.cloned.1.call-start = ((), (), s32[]{:S(2)}) async-start(), calls=%async_computation.16 | async-start | bytes 4718592 | tf_op jit(solution)/shard_map/reduce_scatter | solution.py:167
  472.1 22.1 %copy-start.9 = (f32[256,1024]{1,0:T(8,128)S(1)}, f32[256,1024]{1,0:T(8,128)}, u32[]{:S(2)}) copy-start(f32[256,1024]{1,0:T(8,128)} %all-reduce.11.cloned.1.call-done) | copy-start | bytes 3145732
  (13 other events, 24.0 us)
Sparse Core Ops, SparseCore 0:
  10.6 48.0 all-gather.3
  118.0 40.1 all-reduce.4
  160.5 51.4 all-gather.7
  214.1 47.4 all-gather.5
  267.8 34.5 all-reduce.8
  305.2 33.5 all-reduce.6
  416.0 41.5 all-reduce.10
  461.0 53.8 reduce-scatter.9
  519.3 62.8 reduce-scatter.7
  586.3 74.0 reduce-scatter.5
  664.6 87.1 reduce-scatter.11
  756.3 88.2 reduce-scatter.13
where the time goes:
time: 853 us; the launch traced here: 851 us
  waiting for transfers between devices  636 us (75%)
  blocking collectives  77.8 us (9%)
  matrix products  35.6 us (4%)
  starting transfers between devices  29.3 us (3%)
  local copies, waits for them, and re-layouts  29.2 us (3%)
  between operations  24.6 us (3%)
  other arithmetic  18.9 us (2%)
    reduce_scatter x5, waiting for transfers between devices, local_general(): lax.psum_scatter(v, 'seq', scatter_dimension=d, tiled=True)  348 us
    all_gather x2, blocking collectives, local_general(): cols = lambda v: lax.all_gather(v, 'seq', axis=1, tiled=True)  55.7 us
    all_gather x1, waiting for transfers between devices, local_general(): cols = lambda v: lax.all_gather(v, 'seq', axis=1, tiled=True)  52.1 us
    all_gather x2, waiting for transfers between devices, local_general(): rows = lambda v: lax.all_gather(v, 'seq', axis=0, tiled=True)  46.4 us
    ppermute x12, waiting for transfers between devices, shifted(): lax.ppermute(value, axis, [(i, i + steps) for i in range(first, last)])  42.2 us
    psum x1, waiting for transfers between devices, local_general(): lax.psum(jnp.einsum('tcf,dcf->td', grad_triple, qkv, preferred_element_ty...  41.7 us
    psum x1, waiting for transfers between devices, local_general(): middle = inputs + lax.psum(dot(attended, out_w, ((1,), (0,))), 'head')  38.9 us
    psum x1, waiting for transfers between devices, local_general(): lax.psum(dot(hidden, down_w, ((1,), (0,))).astype(BF16), 'head').astype(F32)  34.6 us
  transfers between devices with their start and end apart: 24, of which 17 were waited for; matrix products, arithmetic and copies ran while one was open for 4% of the time, Pallas kernels for 0%

commit v1 on v0

--- a/solution.py
+++ b/solution.py
@@ -1,3 +1,4 @@
+import functools
 import jax
 import jax.numpy as jnp
 from jax import lax
@@ -11,6 +12,25 @@
 NEGATIVE = -1e30
 F32 = jnp.float32
 BF16 = jnp.bfloat16
+
+
+def define_rings(own_rows, ax_name):
+    n_shards = jax.lax.axis_size(ax_name)
+    table = tuple(((s, (s + 1) % n_shards) for s in range(n_shards)))
+    crops = tuple(((s, (s - 1) % n_shards) for s in range(n_shards)))
+    right_arr, met_up = ([own_rows], [own_rows])
+    for _ in range(n_shards // 2):
+        latest = jax.lax.ppermute(right_arr[-1], axis_name=ax_name, perm=table)
+        right_arr.append(latest)
+    for _ in range((n_shards - 1) // 2):
+        met_up.append(jax.lax.ppermute(met_up[-1], axis_name=ax_name, perm=crops))
+    d_next = jnp.concatenate([*right_arr[::-1], *met_up[1:]], axis=0)
+    return jnp.roll(
+        d_next, shift=(jax.lax.axis_index(ax_name) - n_shards // 2) * own_rows.shape[0], axis=0
+    )
+
+
+_arrange_view = functools.partial(define_rings, ax_name="seq")
 
 
 def shifted(value, axis, steps):
@@ -82,7 +102,7 @@
 ):
     tok, width = tokens.shape
     heads = w_qkv.shape[2] // HEAD_DIM
-    rows = lambda v: lax.all_gather(v, "seq", axis=0, tiled=True)
+    rows = lambda v: _arrange_view(v)
     cols = lambda v: lax.all_gather(v, "seq", axis=1, tiled=True)
     vectors = jnp.stack([ln1_gain, ln1_bias, ln2_gain, ln2_bias, down_bias], axis=0)
     gain_one, shift_one, gain_two, shift_two, down_shift = [

time: 853 us -> 822 us (0.964)
  waiting for transfers between devices: 636 us -> 550 us
  starting transfers between devices: 29.3 us -> 68.5 us
  local copies, waits for them, and re-layouts: 29.2 us -> 42.4 us
    all_gather x1, waiting for transfers between devices: 52.1 us -> 1.25 us  [local_general(): cols = lambda v: lax.all_gather(v, 'seq', axis=1, tiled=True)]
    ppermute x0 -> x14, waiting for transfers between devices: none -> 48.8 us  [the longest x8 47.5 us: define_rings(): latest = jax.lax.ppermute(right_arr[-1], axis_name=ax_name, perm=table)]
    all_gather x2 -> x0, waiting for transfers between devices: 46.4 us -> none  [local_general(): rows = lambda v: lax.all_gather(v, 'seq', axis=0, tiled=True)]
    psum x1, waiting for transfers between devices: 38.9 us -> 0.01 us  [local_general(): middle = inputs + lax.psum(dot(attended, out_w, ((1,), (0,))), 'head')]
    ppermute x0 -> x14, starting transfers between devices: none -> 36.5 us  [the longest x6 22.6 us: define_rings(): met_up.append(jax.lax.ppermute(met_up[-1], axis_name=ax_name, perm=crops))]
    psum x1, waiting for transfers between devices: 41.7 us -> 55.7 us  [local_general(): lax.psum(jnp.einsum('tcf,dcf->td', grad_triple, qkv, preferred_element_ty...]
    unnamed x48 -> x108, local copies, waits for them, and re-layouts: 9.05 us -> 21.5 us
    ppermute x12, waiting for transfers between devices: 42.2 us -> 33.4 us  [shifted(): lax.ppermute(value, axis, [(i, i + steps) for i in range(first, last)])]
  transfers between devices with their start and end apart: 24 -> 36, of which waited for: 17 -> 24; matrix products, arithmetic and copies ran while one was open for 4% -> 5% of each run, Pallas kernels for 0% -> 0%
where the time goes in v1:
time: 822 us; the launch traced here: 820 us
  waiting for transfers between devices  550 us (67%)
  blocking collectives  76.1 us (9%)
  starting transfers between devices  68.5 us (8%)
  local copies, waits for them, and re-layouts  42.4 us (5%)
  matrix products  36.5 us (4%)
  between operations  26 us (3%)
  other arithmetic  20.6 us (3%)
    reduce_scatter x5, waiting for transfers between devices, local_general(): lax.psum_scatter(v, 'seq', scatter_dimension=d, tiled=True)  345 us
    psum x1, waiting for transfers between devices, local_general(): lax.psum(jnp.einsum('tcf,dcf->td', grad_triple, qkv, preferred_element_ty...  55.7 us
    all_gather x2, blocking collectives, local_general(): cols = lambda v: lax.all_gather(v, 'seq', axis=1, tiled=True)  54.2 us
    ppermute x8, waiting for transfers between devices, define_rings(): latest = jax.lax.ppermute(right_arr[-1], axis_name=ax_name, perm=table)  47.5 us
    psum x1, waiting for transfers between devices, local_general(): lax.psum(dot(hidden, down_w, ((1,), (0,))).astype(BF16), 'head').astype(F32)  34.2 us
    ppermute x12, waiting for transfers between devices, shifted(): lax.ppermute(value, axis, [(i, i + steps) for i in range(first, last)])  33.4 us
    psum x1, waiting for transfers between devices, local_general(): grad_two = lax.psum(dot(grad_pre, up_w, ((1,), (1,))), 'head')  31.6 us
    ppermute x12, starting transfers between devices, shifted(): lax.ppermute(value, axis, [(i, i + steps) for i in range(first, last)])  31.3 us
  transfers between devices with their start and end apart: 36, of which 24 were waited for; matrix products, arithmetic and copies ran while one was open for 5% of the time, Pallas kernels for 0%

profile of v1, /device:TPU:0, one launch (start us, length us, event | category | flops | bytes accessed | tf_op | source)
XLA Modules:
  0.0 820.2 jit_solution(11644250693280393498)
XLA Ops:
  24.6 26.0 %all_gather.9 = bf16[5,1024]{1,0:T(8,128)(2,1)S(1)} all-gather(bf16[5,128]{1,0:T(8,128)(2,1)S(1)} %stack.75), channel_id=1, replica_groups=mesh['seq'=8,'head'=4] {'seq'}, dimensions={1}, use_global_device_ids=true | all-gather | bytes 11520 | tf_op jit(solution)/shard_map/all_gather | solution.py:106
  56.3 28.2 %all_gather.10 = bf16[256,1024]{1,0:T(8,128)(2,1)S(1)} all-gather(bf16[256,128]{1,0:T(8,128)(2,1)} %param.17), channel_id=1, replica_groups=mesh['seq'=8,'head'=4] {'seq'}, dimensions={1}, use_global_device_ids=true | all-gather | bytes 589824 | tf_op jit(solution)/shard_map/all_gather | solution.py:106
  86.6 8.3 %collective-permute-done.1 = bf16[128,3,256]{0,2,1:T(8,128)(2,1)S(1)} collective-permute-done((bf16[128,3,256]{0,2,1:T(8,128)(2,1)S(1)}, bf16[128,3,256]{0,2,1:T(8,128)(2,1)S(1)}, u32[]{:S(2)}, u32[]{:S(2)}) %collective-permute-start.1) | collective-permute-done | bytes 196640 | tf_op jit(solution)/shard_map/ppermute | solution.py:23
  95.1 4.8 collective-permute-start.5
  99.9 3.5 collective-permute-done.2
  103.4 4.9 collective-permute-start.6
  128.9 7.8 collective-permute-done.10
  136.7 4.2 collective-permute-done.11
  152.9 5.9 collective-permute-start.13
  158.8 8.7 %collective-permute-done.13 = bf16[128,1024]{1,0:T(8,128)(2,1)S(1)} collective-permute-done((bf16[128,1024]{1,0:T(8,128)(2,1)S(1)}, bf16[128,1024]{1,0:T(8,128)(2,1)S(1)}, u32[]{:S(2)}, u32[]{:S(2)}) %collective-permute-start.13) | collective-permute-done | bytes 262176 | tf_op jit(solution)/shard_map/ppermute | solution.py:23
  172.3 8.6 %collective-permute-done.14 = bf16[128,1024]{1,0:T(8,128)(2,1)S(1)} collective-permute-done((bf16[128,1024]{1,0:T(8,128)(2,1)S(1)}, bf16[128,1024]{1,0:T(8,128)(2,1)S(1)}, u32[]{:S(2)}, u32[]{:S(2)}) %collective-permute-start.14) | collective-permute-done | bytes 262176 | tf_op jit(solution)/shard_map/ppermute | solution.py:23
  186.0 6.8 collective-permute-done.15
  192.8 4.9 collective-permute-start.19
  197.8 8.1 collective-permute-done.16
  222.7 3.7 convert_reduce_fusion.2
  233.9 31.6 %all-reduce.9.cloned.1.call-done = f32[256,1024]{1,0:T(8,128)} async-done(((f32[256,1024]{1,0:T(8,128)}), f32[256,1024]{1,0:T(8,128)}) %all-reduce.9.cloned.1.call-update) | async-done | bytes 1048592 | tf_op jit(solution)/shard_map/psum | solution.py:152
  267.8 34.2 %all-reduce.7.cloned.1.call-done = bf16[256,1024]{1,0:T(8,128)(2,1)} async-done(((bf16[256,1024]{1,0:T(8,128)(2,1)}), bf16[256,1024]{1,0:T(8,128)(2,1)}) %all-reduce.7.cloned.1.call-update) | async-done | bytes 524304 | tf_op jit(solution)/shard_map/psum | solution.py:145
  302.0 3.5 convert_add_fusion.1
  331.3 5.4 collective-permute-start.23
  336.7 4.6 collective-permute-start.24
  341.3 3.8 collective-permute-done.20
  345.1 6.0 collective-permute-start.25
  352.0 3.7 collective-permute-done.21
  355.7 11.6 %collective-permute-done.23 = f32[2,256,256]{2,1,0:T(8,128)} collective-permute-done((f32[2,256,256]{2,1,0:T(8,128)}, f32[2,256,256]{2,1,0:T(8,128)}, u32[]{:S(2)}, u32[]{:S(2)}) %collective-permute-start.23) | collective-permute-done | bytes 524320 | tf_op jit(solution)/shard_map/ppermute | solution.py:39
  371.3 55.7 %all-reduce.11.cloned.1.call-done = f32[256,1024]{1,0:T(8,128)} async-done(((f32[256,1024]{1,0:T(8,128)}), f32[256,1024]{1,0:T(8,128)}) %all-reduce.11.cloned.1.call-update) | async-done | bytes 1048592 | tf_op jit(solution)/shard_map/psum | solution.py:173
  434.8 3.5 fusion.64
  443.3 21.9 %psum.39 = f32[1024]{0:T(1024)} all-reduce(f32[1024]{0:T(1024)S(1)} %copy-done.34), channel_id=1, replica_groups=mesh['seq'=8,'head'=4] {'seq'}, use_global_device_ids=true, to_apply=%region_25.26 | all-reduce | flops 1024 | bytes 8192 | tf_op jit(solution)/shard_map/psum | solution.py:151
  466.6 17.6 %reduce-scatter.10.cloned.1.call-done = f32[5,128]{1,0:T(8,128)} async-done(((f32[5,1024]{1,0:T(8,128)}), f32[5,128]{1,0:T(8,128)}) %reduce-scatter.10.cloned.1.call-update) | async-done | bytes 2576 | tf_op jit(solution)/shard_map/reduce_scatter | solution.py:187
  485.6 66.0 %reduce-scatter.8.cloned.1.call-done = f32[256,128]{1,0:T(8,128)} async-done(((f32[256,1024]{1,0:T(8,128)}), f32[256,128]{1,0:T(8,128)}) %reduce-scatter.8.cloned.1.call-update) | async-done | bytes 131088 | tf_op jit(solution)/shard_map/reduce_scatter | solution.py:187
  551.5 77.8 %reduce-scatter.6.cloned.1.call-done = f32[128,3,256]{2,0,1:T(8,128)} async-done(((f32[1024,3,256]{2,0,1:T(8,128)}), f32[128,3,256]{2,0,1:T(8,128)}) %reduce-scatter.6.cloned.1.call-update) | async-done | bytes 393232 | tf_op jit(solution)/shard_map/reduce_scatter | solution.py:187
  629.4 91.1 %reduce-scatter.12.cloned.1.call-done = f32[128,1024]{1,0:T(8,128)} async-done(((f32[1024,1024]{1,0:T(8,128)}), f32[128,1024]{1,0:T(8,128)}) %reduce-scatter.12.cloned.1.call-update) | async-done | bytes 524304 | tf_op jit(solution)/shard_map/reduce_scatter | solution.py:187
  720.5 92.6 %reduce-scatter.14.cloned.1.call-done = f32[1024,128]{1,0:T(8,128)} async-done(((f32[1024,1024]{1,0:T(8,128)}), f32[1024,128]{1,0:T(8,128)}) %reduce-scatter.14.cloned.1.call-update) | async-done | bytes 524304 | tf_op jit(solution)/shard_map/reduce_scatter | solution.py:187
  (240 shorter events, 129.1 us)
Async XLA Ops:
  8.0 209.4 %all-reduce.5.cloned.1.call-start = ((), (), s32[]{:S(2)}) async-start(), calls=%async_computation.5 | async-start | bytes 2097152 | tf_op jit(solution)/shard_map/psum | solution.py:139
  9.1 77.4 %collective-permute-start = (bf16[128,3,256]{0,2,1:T(8,128)(2,1)S(1)}, bf16[128,3,256]{0,2,1:T(8,128)(2,1)S(1)}, u32[]{:S(2)}, u32[]{:S(2)}) collective-permute-start(bf16[128,3,256]{0,2,1:T(8,128)(2,1)S(1)} %copy.39), channel_id=1, source_target_pairs={{0,4},{4,8},{8,12},{12,16},{16,20},{20,24},{24,28},{28,0},{1,5},{5... | collective-permute-start | bytes 589832 | tf_op jit(solution)/shard_map/ppermute | solution.py:23
  12.2 82.9 %collective-permute-start.4 = (bf16[128,3,256]{0,2,1:T(8,128)(2,1)S(1)}, bf16[128,3,256]{0,2,1:T(8,128)(2,1)S(1)}, u32[]{:S(2)}, u32[]{:S(2)}) collective-permute-start(bf16[128,3,256]{0,2,1:T(8,128)(2,1)S(1)} %copy.39), channel_id=1, source_target_pairs={{0,28},{4,0},{8,4},{12,8},{16,12},{20,16},{24,20},{28,24},{1,29},{... | collective-permute-start | bytes 589832 | tf_op jit(solution)/shard_map/ppermute | solution.py:26
  86.5 8.5 %collective-permute-start.1 = (bf16[128,3,256]{0,2,1:T(8,128)(2,1)S(1)}, bf16[128,3,256]{0,2,1:T(8,128)(2,1)S(1)}, u32[]{:S(2)}, u32[]{:S(2)}) collective-permute-start(bf16[128,3,256]{0,2,1:T(8,128)(2,1)S(1)} %collective-permute-done), channel_id=1, source_target_pairs={{0,4},{4,8},{8,12},{12,16},{16,20},{20,24},{24,28},{28,0},{1,5},{5... | collective-permute-start | bytes 589832 | tf_op jit(solution)/shard_map/ppermute | solution.py:23
  103.4 10.2 %collective-permute-start.6 = (bf16[128,3,256]{0,2,1:T(8,128)(2,1)S(1)}, bf16[128,3,256]{0,2,1:T(8,128)(2,1)S(1)}, u32[]{:S(2)}, u32[]{:S(2)}) collective-permute-start(bf16[128,3,256]{0,2,1:T(8,128)(2,1)S(1)} %collective-permute-done.5), channel_id=1, source_target_pairs={{0,28},{4,0},{8,4},{12,8},{16,12},{20,16},{24,20},{28,24},{1,29},{... | collective-permute-start | bytes 589832 | tf_op jit(solution)/shard_map/ppermute | solution.py:26
  116.7 10.5 %collective-permute-start.7 = (bf16[2,256,256]{1,2,0:T(8,128)(2,1)S(1)}, bf16[2,256,256]{1,2,0:T(8,128)(2,1)S(1)}, u32[]{:S(2)}, u32[]{:S(2)}) collective-permute-start(bf16[2,256,256]{1,2,0:T(8,128)(2,1)S(1)} %pad_maximum_fusion.1), channel_id=1, source_target_pairs={{0,12},{4,16},{8,20},{12,24},{16,28},{1,13},{5,17},{9,21},{13,25},... | collective-permute-start | bytes 786440 | tf_op jit(solution)/shard_map/ppermute | solution.py:39
  120.1 8.4 %collective-permute-start.8 = (bf16[2,256,256]{1,2,0:T(8,128)(2,1)S(1)}, bf16[2,256,256]{1,2,0:T(8,128)(2,1)S(1)}, u32[]{:S(2)}, u32[]{:S(2)}) collective-permute-start(bf16[2,256,256]{1,2,0:T(8,128)(2,1)S(1)} %pad_maximum_fusion.1), channel_id=1, source_target_pairs={{0,8},{4,12},{8,16},{12,20},{16,24},{20,28},{1,9},{5,13},{9,17},{1... | collective-permute-start | bytes 786440 | tf_op jit(solution)/shard_map/ppermute | solution.py:39
  124.5 12.2 %collective-permute-start.10 = (bf16[2,256,256]{1,2,0:T(8,128)(2,1)S(1)}, bf16[2,256,256]{1,2,0:T(8,128)(2,1)S(1)}, u32[]{:S(2)}, u32[]{:S(2)}) collective-permute-start(bf16[2,256,256]{1,2,0:T(8,128)(2,1)S(1)} %pad_maximum_fusion.1), channel_id=1, source_target_pairs={{4,0},{8,4},{12,8},{16,12},{20,16},{24,20},{28,24},{5,1},{9,5},{13... | collective-permute-start | bytes 786440 | tf_op jit(solution)/shard_map/ppermute | solution.py:39
  125.8 15.1 %collective-permute-start.11 = (bf16[2,256,256]{1,2,0:T(8,128)(2,1)S(1)}, bf16[2,256,256]{1,2,0:T(8,128)(2,1)S(1)}, u32[]{:S(2)}, u32[]{:S(2)}) collective-permute-start(bf16[2,256,256]{1,2,0:T(8,128)(2,1)S(1)} %pad_maximum_fusion.1), channel_id=1, source_target_pairs={{8,0},{12,4},{16,8},{20,12},{24,16},{28,20},{9,1},{13,5},{17,9},{2... | collective-permute-start | bytes 786440 | tf_op jit(solution)/shard_map/ppermute | solution.py:39
  127.1 15.7 %collective-permute-start.12 = (bf16[2,256,256]{1,2,0:T(8,128)(2,1)S(1)}, bf16[2,256,256]{1,2,0:T(8,128)(2,1)S(1)}, u32[]{:S(2)}, u32[]{:S(2)}) collective-permute-start(bf16[2,256,256]{1,2,0:T(8,128)(2,1)S(1)} %pad_maximum_fusion.1), channel_id=1, source_target_pairs={{12,0},{16,4},{20,8},{24,12},{28,16},{13,1},{17,5},{21,9},{25,13},... | collective-permute-start | bytes 786440 | tf_op jit(solution)/shard_map/ppermute | solution.py:39
  152.8 67.6 %all-gather.2.cloned.1.call-start = ((), (), s32[]{:S(2)}) async-start(), calls=%async_computation.6 | async-start | bytes 2359296 | tf_op jit(solution)/shard_map/all_gather | solution.py:106
  152.9 14.7 %collective-permute-start.13 = (bf16[128,1024]{1,0:T(8,128)(2,1)S(1)}, bf16[128,1024]{1,0:T(8,128)(2,1)S(1)}, u32[]{:S(2)}, u32[]{:S(2)}) collective-permute-start(bf16[128,1024]{1,0:T(8,128)(2,1)S(1)} %copy-done.14), channel_id=1, source_target_pairs={{0,4},{4,8},{8,12},{12,16},{16,20},{20,24},{24,28},{28,0},{1,5},{5... | collective-permute-start | bytes 786440 | tf_op jit(solution)/shard_map/ppermute | solution.py:23
  158.8 106.7 %all-reduce.9.cloned.1.call-start = ((), (), s32[]{:S(2)}) async-start(), calls=%async_computation.8 | async-start | bytes 2097152 | tf_op jit(solution)/shard_map/psum | solution.py:152
  167.6 13.4 %collective-permute-start.14 = (bf16[128,1024]{1,0:T(8,128)(2,1)S(1)}, bf16[128,1024]{1,0:T(8,128)(2,1)S(1)}, u32[]{:S(2)}, u32[]{:S(2)}) collective-permute-start(bf16[128,1024]{1,0:T(8,128)(2,1)S(1)} %collective-permute-done.13), channel_id=1, source_target_pairs={{0,4},{4,8},{8,12},{12,16},{16,20},{20,24},{24,28},{28,0},{1,5},{5... | collective-permute-start | bytes 786440 | tf_op jit(solution)/shard_map/ppermute | solution.py:23
  170.0 13.4 %collective-permute-start.17 = (bf16[128,1024]{1,0:T(8,128)(2,1)S(1)}, bf16[128,1024]{1,0:T(8,128)(2,1)S(1)}, u32[]{:S(2)}, u32[]{:S(2)}) collective-permute-start(bf16[128,1024]{1,0:T(8,128)(2,1)S(1)} %copy-done.14), channel_id=1, source_target_pairs={{0,28},{4,0},{8,4},{12,8},{16,12},{20,16},{24,20},{28,24},{1,29},{... | collective-permute-start | bytes 786440 | tf_op jit(solution)/shard_map/ppermute | solution.py:26
  180.9 11.9 %collective-permute-start.15 = (bf16[128,1024]{1,0:T(8,128)(2,1)S(1)}, bf16[128,1024]{1,0:T(8,128)(2,1)S(1)}, u32[]{:S(2)}, u32[]{:S(2)}) collective-permute-start(bf16[128,1024]{1,0:T(8,128)(2,1)S(1)} %collective-permute-done.14), channel_id=1, source_target_pairs={{0,4},{4,8},{8,12},{12,16},{16,20},{20,24},{24,28},{28,0},{1,5},{5... | collective-permute-start | bytes 786440 | tf_op jit(solution)/shard_map/ppermute | solution.py:23
  183.4 9.4 %collective-permute-start.18 = (bf16[128,1024]{1,0:T(8,128)(2,1)S(1)}, bf16[128,1024]{1,0:T(8,128)(2,1)S(1)}, u32[]{:S(2)}, u32[]{:S(2)}) collective-permute-start(bf16[128,1024]{1,0:T(8,128)(2,1)S(1)} %collective-permute-done.17), channel_id=1, source_target_pairs={{0,28},{4,0},{8,4},{12,8},{16,12},{20,16},{24,20},{28,24},{1,29},{... | collective-permute-start | bytes 786440 | tf_op jit(solution)/shard_map/ppermute | solution.py:26
  192.8 13.0 %collective-permute-start.16 = (bf16[128,1024]{1,0:T(8,128)(2,1)S(1)}, bf16[128,1024]{1,0:T(8,128)(2,1)S(1)}, u32[]{:S(2)}, u32[]{:S(2)}) collective-permute-start(bf16[128,1024]{1,0:T(8,128)(2,1)S(1)} %collective-permute-done.15), channel_id=1, source_target_pairs={{0,4},{4,8},{8,12},{12,16},{16,20},{20,24},{24,28},{28,0},{1,5},{5... | collective-permute-start | bytes 786440 | tf_op jit(solution)/shard_map/ppermute | solution.py:23
  192.8 18.1 %collective-permute-start.19 = (bf16[128,1024]{1,0:T(8,128)(2,1)S(1)}, bf16[128,1024]{1,0:T(8,128)(2,1)S(1)}, u32[]{:S(2)}, u32[]{:S(2)}) collective-permute-start(bf16[128,1024]{1,0:T(8,128)(2,1)S(1)} %collective-permute-done.18), channel_id=1, source_target_pairs={{0,28},{4,0},{8,4},{12,8},{16,12},{20,16},{24,20},{28,24},{1,29},{... | collective-permute-start | bytes 786440 | tf_op jit(solution)/shard_map/ppermute | solution.py:26
  230.5 71.4 %all-reduce.7.cloned.1.call-start = ((), (), s32[]{:S(2)}) async-start(), calls=%async_computation.7 | async-start | bytes 1048576 | tf_op jit(solution)/shard_map/psum | solution.py:145
  233.8 193.2 %all-reduce.11.cloned.1.call-start = ((), (), s32[]{:S(2)}) async-start(), calls=%async_computation.9 | async-start | bytes 2097152 | tf_op jit(solution)/shard_map/psum | solution.py:173
  327.4 17.7 %collective-permute-start.20 = (f32[2,256,256]{2,1,0:T(8,128)S(1)}, f32[2,256,256]{2,1,0:T(8,128)S(1)}, u32[]{:S(2)}, u32[]{:S(2)}) collective-permute-start(f32[2,256,256]{2,1,0:T(8,128)S(1)} %get-tuple-element.24), channel_id=1, source_target_pairs={{12,0},{16,4},{20,8},{24,12},{28,16},{13,1},{17,5},{21,9},{25,13},... | collective-permute-start | bytes 1572872 | tf_op jit(solution)/shard_map/ppermute | solution.py:39
  328.7 27.0 %collective-permute-start.21 = (f32[2,256,256]{2,1,0:T(8,128)}, f32[2,256,256]{2,1,0:T(8,128)}, u32[]{:S(2)}, u32[]{:S(2)}) collective-permute-start(f32[2,256,256]{2,1,0:T(8,128)} %get-tuple-element.29), channel_id=1, source_target_pairs={{8,0},{12,4},{16,8},{20,12},{24,16},{28,20},{9,1},{13,5},{17,9},{2... | collective-permute-start | bytes 1572872 | tf_op jit(solution)/shard_map/ppermute | solution.py:39
  330.0 25.7 %collective-permute-start.22 = (f32[2,256,256]{2,1,0:T(8,128)}, f32[2,256,256]{2,1,0:T(8,128)}, u32[]{:S(2)}, u32[]{:S(2)}) collective-permute-start(f32[2,256,256]{2,1,0:T(8,128)} %get-tuple-element.28), channel_id=1, source_target_pairs={{4,0},{8,4},{12,8},{16,12},{20,16},{24,20},{28,24},{5,1},{9,5},{13... | collective-permute-start | bytes 1572872 | tf_op jit(solution)/shard_map/ppermute | solution.py:39
  331.3 36.0 %collective-permute-start.23 = (f32[2,256,256]{2,1,0:T(8,128)}, f32[2,256,256]{2,1,0:T(8,128)}, u32[]{:S(2)}, u32[]{:S(2)}) collective-permute-start(f32[2,256,256]{2,1,0:T(8,128)} %get-tuple-element.27), channel_id=1, source_target_pairs={{0,4},{4,8},{8,12},{12,16},{16,20},{20,24},{24,28},{1,5},{5,9},{9,... | collective-permute-start | bytes 1572872 | tf_op jit(solution)/shard_map/ppermute | solution.py:39
  336.7 30.6 %collective-permute-start.24 = (f32[2,256,256]{2,1,0:T(8,128)}, f32[2,256,256]{2,1,0:T(8,128)}, u32[]{:S(2)}, u32[]{:S(2)}) collective-permute-start(f32[2,256,256]{2,1,0:T(8,128)} %get-tuple-element.26), channel_id=1, source_target_pairs={{0,8},{4,12},{8,16},{12,20},{16,24},{20,28},{1,9},{5,13},{9,17},{1... | collective-permute-start | bytes 1572872 | tf_op jit(solution)/shard_map/ppermute | solution.py:39
  345.1 22.2 %collective-permute-start.25 = (f32[2,256,256]{2,1,0:T(8,128)}, f32[2,256,256]{2,1,0:T(8,128)}, u32[]{:S(2)}, u32[]{:S(2)}) collective-permute-start(f32[2,256,256]{2,1,0:T(8,128)} %get-tuple-element.25), channel_id=1, source_target_pairs={{0,12},{4,16},{8,20},{12,24},{16,28},{1,13},{5,17},{9,21},{13,25},... | collective-permute-start | bytes 1572872 | tf_op jit(solution)/shard_map/ppermute | solution.py:39
  371.0 113.1 %reduce-scatter.10.cloned.1.call-start = ((), (), s32[]{:S(2)}) async-start(), calls=%async_computation.12 | async-start | bytes 36864 | tf_op jit(solution)/shard_map/reduce_scatter | solution.py:187
  430.1 121.5 %reduce-scatter.8.cloned.1.call-start = ((), (), s32[]{:S(2)}) async-start(), calls=%async_computation.11 | async-start | bytes 1179648 | tf_op jit(solution)/shard_map/reduce_scatter | solution.py:187
  431.5 197.9 %reduce-scatter.6.cloned.1.call-start = ((), (), s32[]{:S(2)}) async-start(), calls=%async_computation.10 | async-start | bytes 3538944 | tf_op jit(solution)/shard_map/reduce_scatter | solution.py:187
  434.7 285.8 %reduce-scatter.12.cloned.1.call-start = ((), (), s32[]{:S(2)}) async-start(), calls=%async_computation.13 | async-start | bytes 4718592 | tf_op jit(solution)/shard_map/reduce_scatter | solution.py:187
  438.3 374.8 %reduce-scatter.14.cloned.1.call-start = ((), (), s32[]{:S(2)}) async-start(), calls=%async_computation.14 | async-start | bytes 4718592 | tf_op jit(solution)/shard_map/reduce_scatter | solution.py:187
  (40 other events, 855.9 us)
Sparse Core Ops, SparseCore 0:
  152.9 38.7 all-reduce.4
  230.6 34.7 all-reduce.8
  268.4 33.5 all-reduce.6
  371.1 55.8 all-reduce.10
Sparse Core Ops, SparseCore 1:
  158.9 61.5 all-gather.1
  430.1 54.0 reduce-scatter.9
  488.4 63.1 reduce-scatter.7
  555.7 73.6 reduce-scatter.5
  633.6 86.8 reduce-scatter.11
  725.2 87.9 reduce-scatter.13
